TPU v7x, 32 devices: a whole 2x2x4 slice. The times are simulated.
32 devices in a mesh: member: 2 (over y), lon: 4 (over z), lat: 2 (over x), dp: 2 (over core).
Axes of the slice: x: 2, y: 2, z: 4, core: 2. Of those that a mesh axis runs over, the one named last changes fastest.
Arguments:
- fields: bfloat16 [4, 64, 32, 512], P(('member', 'dp'), 'lat', 'lon'), parts along dimension 0, may hold values from -6 to 6
- cotangent: bfloat16 [4, 64, 32, 512], P(('member', 'dp'), 'lat', 'lon'), parts along dimension 0, may hold values from -6 to 6
- conv_weight: float32 [7, 7, 512], replicated, may hold values from -0.875 to 0.875
- norm_gain: float32 [512], replicated, may hold values from 0.1 to 1.9
- w_qkv: bfloat16 [512, 768], replicated, may hold values from -1 to 1
- w_out: bfloat16 [256, 512], replicated, may hold values from -0.375 to 0.375
Outputs:
- result: bfloat16 [4, 64, 32, 512], P(('member', 'dp'), 'lat', 'lon'), parts along dimension 0
- grad_fields: bfloat16 [4, 64, 32, 512], P(('member', 'dp'), 'lat', 'lon'), parts along dimension 0
- grad_qkv: float32 [1024, 768], P('member'), parts along dimension 0
- grad_out: float32 [512, 512], P('member'), parts along dimension 0
- grad_conv: float32 [14, 7, 512], P('member'), parts along dimension 0
- grad_gain: float32 [1024], P('member'), parts along dimension 0
There are 2 independent parts, one for each index of `member`. A program takes and returns all parts, laid end to end along the dimension named above; an argument that names none is the same for every part. Nothing has to cross between parts.
All inputs are finite; a program needn't handle non-finite values.
Results may differ from a plain program's by a relative error of at most 0.012.
The roundings to bfloat16 on the way count: a program that leaves them out, or rounds other values in their place, can miss the bound.
Values may be sent and summed in bfloat16 or wider, within the bound.
A program may use at most 64 MiB of HBM per device.

v0:
```python
import jax
import jax.numpy as jnp
from jax import lax
from jax.sharding import PartitionSpec as P

HEADS = 4
HEAD_DIM = 64
EPSILON = 1e-06


def with_halo(x, sides, width, wrap):
    for axis, dim in sides:
        size, length = (lax.axis_size(axis), x.shape[dim])
        up = [(i, (i + 1) % size) for i in range(size if wrap else size - 1)]
        down = [(j, i) for i, j in up]
        last = lax.slice_in_dim(x, length - width, length, axis=dim)
        first = lax.slice_in_dim(x, 0, width, axis=dim)
        before = lax.ppermute(last, axis, up)
        after = lax.ppermute(first, axis, down)
        x = jnp.concatenate([before, x, after], axis=dim)
    return x


def spread(padded, kernel, lat_rows, lon_cols):
    summed = jnp.zeros(padded.shape[:1] + (lat_rows, lon_cols, padded.shape[3]), jnp.float32)
    for row_shift in range(7):
        band = padded[:, row_shift : row_shift + lat_rows].astype(jnp.float32)
        partial_row = kernel[row_shift, 0] * band[:, :, 0:lon_cols]
        for col_shift in range(1, 7):
            partial_row = (
                partial_row
                + kernel[row_shift, col_shift] * band[:, :, col_shift : col_shift + lon_cols]
            )
        summed = summed + partial_row
    return summed


def correlate(padded, upstream, lat_rows, lon_cols):
    pieces = []
    for row_shift in range(7):
        for col_shift in range(7):
            window = padded[
                :, row_shift : row_shift + lat_rows, col_shift : col_shift + lon_cols
            ].astype(jnp.float32)
            pieces.append(jnp.sum(window * upstream, axis=(0, 1, 2)))
    return jnp.stack(pieces).reshape(7, 7, -1)


def split_heads(values):
    return values.reshape(values.shape[:-1] + (HEADS, HEAD_DIM))


def attend_forward(rowwise, att_width):
    queries = split_heads(rowwise[..., :att_width])
    keys_part = split_heads(rowwise[..., att_width : 2 * att_width])
    values_part = split_heads(rowwise[..., 2 * att_width :])
    scores = jnp.einsum(
        "brqhd,brkhd->brhqk", queries, keys_part, preferred_element_type=jnp.float32
    ) * HEAD_DIM ** (-0.5)
    row_peak = jnp.max(scores, -1, keepdims=True)
    raised = jnp.exp(scores - row_peak)
    probs = raised / jnp.sum(raised, -1, keepdims=True)
    weights = probs.astype(jnp.bfloat16)
    mixed = jnp.einsum(
        "brhqk,brkhd->brqhd", weights, values_part, preferred_element_type=jnp.float32
    )
    return (mixed.reshape(rowwise.shape[:3] + (att_width,)).astype(jnp.bfloat16), probs)


def attend_backward(rowwise, probs, grad_rowwise, att_width):
    queries = split_heads(rowwise[..., :att_width])
    keys_part = split_heads(rowwise[..., att_width : 2 * att_width])
    values_part = split_heads(rowwise[..., 2 * att_width :])
    grad_heads = split_heads(grad_rowwise)
    weights = probs.astype(jnp.bfloat16)
    grad_probs = jnp.einsum(
        "brqhd,brkhd->brhqk", grad_heads, values_part, preferred_element_type=jnp.float32
    )
    inner = jnp.sum(probs * grad_probs, -1, keepdims=True)
    grad_scores = (probs * (grad_probs - inner) * HEAD_DIM ** (-0.5)).astype(jnp.bfloat16)
    grad_query = jnp.einsum(
        "brhqk,brkhd->brqhd", grad_scores, keys_part, preferred_element_type=jnp.float32
    )
    grad_key = jnp.einsum(
        "brhqk,brqhd->brkhd", grad_scores, queries, preferred_element_type=jnp.float32
    )
    grad_value = jnp.einsum(
        "brhqk,brqhd->brkhd", weights, grad_heads, preferred_element_type=jnp.float32
    )
    shaped = rowwise.shape[:3] + (att_width,)
    return jnp.concatenate(
        [
            grad_query.reshape(shaped).astype(jnp.bfloat16),
            grad_key.reshape(shaped).astype(jnp.bfloat16),
            grad_value.reshape(shaped).astype(jnp.bfloat16),
        ],
        axis=-1,
    )


def contract_rows(left, right):
    return lax.dot_general(
        left, right, (((0,), (0,)), ((), ())), preferred_element_type=jnp.float32
    )


def contract_cols(left, right):
    return lax.dot_general(
        left, right, (((1,), (1,)), ((), ())), preferred_element_type=jnp.float32
    )


def on_device(fields, cotangent, conv_weight, norm_gain, w_qkv, w_out):
    batch_count, lat_rows, lon_cols, channels = fields.shape
    att_width = w_out.shape[0]
    wide = with_halo(fields, (("lon", 2),), 3, True)
    padded = with_halo(wide, (("lat", 1),), 3, False)
    update = fields.astype(jnp.float32) + spread(padded, conv_weight, lat_rows, lon_cols)
    inverse = lax.rsqrt(jnp.mean(update * update, -1, keepdims=True) + EPSILON)
    normed = (update * inverse * norm_gain).astype(jnp.bfloat16)
    normed_flat = normed.reshape(-1, channels)
    projected = jnp.dot(normed_flat, w_qkv, preferred_element_type=jnp.float32).astype(jnp.bfloat16)
    rowwise = lax.all_to_all(
        projected.reshape(batch_count, lat_rows, lon_cols, 3 * att_width),
        "lon",
        split_axis=1,
        concat_axis=2,
        tiled=True,
    )
    mixed_rows, probs = attend_forward(rowwise, att_width)
    mixed = lax.all_to_all(mixed_rows, "lon", split_axis=2, concat_axis=1, tiled=True)
    mixed_flat = mixed.reshape(-1, att_width)
    result = (
        update
        + jnp.dot(mixed_flat, w_out, preferred_element_type=jnp.float32).reshape(update.shape)
    ).astype(jnp.bfloat16)
    upstream_flat = cotangent.reshape(-1, channels)
    grad_mixed = contract_cols(upstream_flat, w_out).astype(jnp.bfloat16)
    grad_out = contract_rows(mixed_flat, upstream_flat)
    grad_rowwise = lax.all_to_all(
        grad_mixed.reshape(batch_count, lat_rows, lon_cols, att_width),
        "lon",
        split_axis=1,
        concat_axis=2,
        tiled=True,
    )
    grad_projected_rows = attend_backward(rowwise, probs, grad_rowwise, att_width)
    grad_projected = lax.all_to_all(
        grad_projected_rows, "lon", split_axis=2, concat_axis=1, tiled=True
    )
    grad_flat = grad_projected.reshape(-1, 3 * att_width)
    grad_weight = contract_rows(normed_flat, grad_flat)
    grad_normed = contract_cols(grad_flat, w_qkv).reshape(update.shape)
    grad_gain = jnp.sum(grad_normed * (update * inverse), axis=(0, 1, 2))
    gained = norm_gain * grad_normed
    grad_update = (
        cotangent.astype(jnp.float32)
        + inverse * gained
        - update * inverse**3 * jnp.mean(gained * update, -1, keepdims=True)
    )
    grad_wide = with_halo(grad_update.astype(jnp.bfloat16), (("lon", 2),), 3, True).astype(
        grad_update.dtype
    )
    grad_padded = with_halo(grad_wide.astype(jnp.bfloat16), (("lat", 1),), 3, False).astype(
        grad_wide.dtype
    )
    grad_fields = (
        grad_update + spread(grad_padded, conv_weight[::-1, ::-1], lat_rows, lon_cols)
    ).astype(jnp.bfloat16)
    grad_conv = correlate(padded, grad_update, lat_rows, lon_cols)
    totals = lax.psum((grad_weight, grad_out, grad_conv, grad_gain), ("lon", "lat", "dp"))
    return (result, grad_fields, totals[0], totals[1], totals[2], totals[3])


def solution(mesh):
    placed = (
        P(("member", "dp"), "lat", "lon", None),
        P(("member", "dp"), "lat", "lon", None),
        P(),
        P(),
        P(),
        P(),
    )
    return jax.shard_map(
        on_device,
        mesh=mesh,
        in_specs=placed,
        out_specs=(
            P(("member", "dp"), "lat", "lon", None),
            P(("member", "dp"), "lat", "lon", None),
            P("member", None),
            P("member", None),
            P("member", None, None),
            P("member"),
        ),
        check_vma=False,
    )
```

profile of v0, /device:TPU:0, one launch (start us, length us, event | category | flops | bytes accessed | tf_op | source)
XLA Modules:
  0.0 233.1 jit_solution(6971295654083758024)
XLA Ops:
  8.4 3.1 %collective-permute-start = (bf16[1,32,3,512]{3,2,1,0:T(4,128)(2,1)S(1)}, bf16[1,32,3,512]{3,2,1,0:T(4,128)(2,1)S(1)}, u32[]{:S(2)}, u32[]{:S(2)}) collective-permute-start(bf16[1,32,3,512]{3,2,1,0:T(4,128)(2,1)S(1)} %get-tuple-element.93), channel_id=1, source_target_pairs={{0,4},{4,8},{8,12},{12,0},{1,5},{5,9},{9,13},{13,1},{2,6},{6,10},{... | collective-permute-start | bytes 294920 | tf_op jit(solution)/shard_map/ppermute | solution.py:18
  11.6 2.1 collective-permute-start.1
  13.6 1.9 fusion.15
  15.6 3.9 %all-to-all-start.2 = ((bf16[1,32,8,256]{3,2,0,1:T(8,128)(2,1)}), bf16[1,32,8,256]{3,2,0,1:T(8,128)(2,1)}, u32[]{:S(2)}, u32[]{:S(2)}) async-start(bf16[1,32,8,256]{3,2,0,1:T(8,128)(2,1)} %fusion.15), calls=%async_computation.2 | async-start | bytes 262144 | tf_op jit(solution)/shard_map/all_to_all | solution.py:140
  22.1 3.5 %collective-permute-start.2 = (bf16[1,3,14,512]{3,2,1,0:T(8,128)(2,1)S(1)}, bf16[1,3,14,512]{3,2,1,0:T(8,128)(2,1)S(1)}, u32[]{:S(2)}, u32[]{:S(2)}) collective-permute-start(bf16[1,3,14,512]{3,2,1,0:T(8,128)(2,1)S(1)} %get-tuple-element.84), channel_id=1, source_target_pairs={{0,2},{1,3},{4,6},{5,7},{8,10},{9,11},{12,14},{13,15},{16,18},{17,... | collective-permute-start | bytes 129032 | tf_op jit(solution)/shard_map/ppermute | solution.py:18
  27.6 4.0 %collective-permute-done.3 = bf16[1,3,14,512]{3,2,1,0:T(8,128)(2,1)S(1)} collective-permute-done((bf16[1,3,14,512]{3,2,1,0:T(8,128)(2,1)S(1)}, bf16[1,3,14,512]{3,2,1,0:T(8,128)(2,1)S(1)}, u32[]{:S(2)}, u32[]{:S(2)}) %collective-permute-start.3) | collective-permute-done | bytes 43040 | tf_op jit(solution)/shard_map/ppermute | solution.py:19
  32.0 2.0 slice_convert_fusion.2
  34.0 10.5 %multiply_reduce_fusion.51 = (f32[32,8]{1,0:T(8,128)S(1)}, f32[1,32,8,512]{3,2,1,0:T(8,128)S(1)}) fusion(f32[1,32,14,512]{3,2,1,0:T(8,128)S(1)} %get-tuple-element.77, f32[512]{0:T(512)} %bitcast.283, f32[512]{0:T(512)} %bitcast.285, f32[512]{0:T(512)S(1)} %bitcast.191, f32[512]{0:T(512)S(1)} %bitcast.193, f32[512]{0:T(512)S(1)} %bitcast.195, ...), kind=kLoop, calls=%fused_computation.293 | loop fusion | flops 13238016 | bytes 26577920 | tf_op jit(solution)/shard_map/reduce_sum | solution.py:119
  45.7 5.0 %all-to-all-start = ((bf16[1,32,8,768]{3,2,0,1:T(8,128)(2,1)}), bf16[1,32,8,768]{3,2,0,1:T(8,128)(2,1)S(1)}, u32[]{:S(2)}, u32[]{:S(2)}) async-start(bf16[1,32,8,768]{3,2,0,1:T(8,128)(2,1)} %fusion.10), calls=%async_computation | async-start | bytes 786432 | tf_op jit(solution)/shard_map/all_to_all | solution.py:123
  54.2 6.2 %all-to-all-done = bf16[1,32,8,768]{3,2,0,1:T(8,128)(2,1)S(1)} async-done(((bf16[1,32,8,768]{3,2,0,1:T(8,128)(2,1)}), bf16[1,32,8,768]{3,2,0,1:T(8,128)(2,1)S(1)}, u32[]{:S(2)}, u32[]{:S(2)}) %all-to-all-start) | async-done | bytes 393248 | tf_op jit(solution)/shard_map/all_to_all | solution.py:123
  62.3 2.1 fusion.164
  65.5 2.0 fusion.14
  68.6 2.6 %fusion.12 = bf16[1,8,32,4,64]{4,2,3,1,0:T(8,128)(2,1)} fusion(f32[8,4,32,32]{2,3,1,0:T(8,128)} %fusion.129, bf16[8,32,4,64]{3,2,1,0:T(4,128)(2,1)S(1)} %copy-done.18, f32[8,4,32,32]{2,3,1,0:T(8,128)} %get-tuple-element.147, f32[8,4,32]{2,1,0:T(4,128)S(1)} %get-tuple-element.146), kind=kOutput, calls=%fused_computation.20 | convolution fusion | flops 4490271 | bytes 528384 | tf_op jit(solution)/shard_map/brhqk,brkhd->brqhd/dot_general | solution.py:81
  75.1 3.9 %all-to-all-start.1 = ((bf16[1,8,32,256]{3,1,0,2:T(8,128)(2,1)}), bf16[1,8,32,256]{3,1,0,2:T(8,128)(2,1)}, u32[]{:S(2)}, u32[]{:S(2)}) async-start(bf16[1,8,32,256]{3,1,0,2:T(8,128)(2,1)} %reshape.619), calls=%async_computation.1 | async-start | bytes 262144 | tf_op jit(solution)/shard_map/all_to_all | solution.py:131
  79.1 2.6 %fusion.13 = bf16[1,8,32,4,64]{4,2,3,1,0:T(8,128)(2,1)} fusion(f32[8,4,32,32]{2,3,1,0:T(8,128)} %fusion.129, bf16[8,32,4,64]{3,2,1,0:T(4,128)(2,1)S(1)} %copy-done.17, f32[8,4,32,32]{2,3,1,0:T(8,128)} %get-tuple-element.147, f32[8,4,32]{2,1,0:T(4,128)S(1)} %get-tuple-element.146), kind=kOutput, calls=%fused_computation.21 | convolution fusion | flops 4490271 | bytes 528384 | tf_op jit(solution)/shard_map/brhqk,brqhd->brkhd/dot_general | solution.py:84
  87.6 5.0 %all-to-all-start.3 = ((bf16[1,8,32,768]{3,1,0,2:T(8,128)(2,1)}), bf16[1,8,32,768]{3,1,0,2:T(8,128)(2,1)S(1)}, u32[]{:S(2)}, u32[]{:S(2)}) async-start(bf16[1,8,32,768]{3,1,0,2:T(8,128)(2,1)} %copy.93), calls=%async_computation.3 | async-start | bytes 786432 | tf_op jit(solution)/shard_map/all_to_all | solution.py:148
  97.3 4.3 %all-to-all-done.3 = bf16[1,8,32,768]{3,1,0,2:T(8,128)(2,1)S(1)} async-done(((bf16[1,8,32,768]{3,1,0,2:T(8,128)(2,1)}), bf16[1,8,32,768]{3,1,0,2:T(8,128)(2,1)S(1)}, u32[]{:S(2)}, u32[]{:S(2)}) %all-to-all-start.3) | async-done | bytes 393248 | tf_op jit(solution)/shard_map/all_to_all | solution.py:148
  102.7 2.2 multiply_reduce_fusion.2
  104.9 2.0 multiply_reduce_fusion.29
  107.6 3.3 %collective-permute-start.5 = (bf16[1,32,3,512]{3,2,1,0:T(4,128)(2,1)S(1)}, bf16[1,32,3,512]{3,2,1,0:T(4,128)(2,1)S(1)}, u32[]{:S(2)}, u32[]{:S(2)}) collective-permute-start(bf16[1,32,3,512]{3,2,1,0:T(4,128)(2,1)S(1)} %get-tuple-element.92), channel_id=1, source_target_pairs={{4,0},{8,4},{12,8},{0,12},{5,1},{9,5},{13,9},{1,13},{6,2},{10,6},{... | collective-permute-start | bytes 294920 | tf_op jit(solution)/shard_map/ppermute | solution.py:19
  121.2 31.5 %psum.31 = f32[512]{0:T(512)} all-reduce(f32[512]{0:T(512)S(1)} %copy-done.93), channel_id=1, replica_groups=mesh['member'=2,'lon'=4,'lat'=2,'dp'=2] {'lon','lat','dp'}, use_global_device_ids=true, to_apply=%region_58.0 | all-reduce | flops 512 | bytes 4096 | tf_op jit(solution)/shard_map/psum | solution.py:171
  153.3 4.5 %fusion.24 = bf16[1,32,8,512]{3,2,1,0:T(8,128)(2,1)} fusion(f32[1,32,8,512]{3,2,1,0:T(8,128)S(1)} %get-tuple-element.70, f32[1,38,14,512]{3,2,1,0:T(8,128)S(1)} %maximum_convert_fusion, f32[512]{0:T(512)S(1)} %bitcast.284, f32[512]{0:T(512)S(1)} %bitcast.286, f32[512]{0:T(512)S(1)} %bitcast.192, f32[512]{0:T(512)S(1)} %bitcast.194, f32[512]{0:T(512)S(1)} %bitcast.196, ...), kind=kLoop, calls=%fused_computation.42 | loop fusion | flops 12976128 | bytes 26576896 | tf_op jit(solution)/shard_map/convert_element_type | solution.py:169
  157.8 64.3 %all-reduce.3.cloned.1.call-done = (f32[512,768]{1,0:T(8,128)}, f32[256,512]{1,0:T(8,128)}, f32[7,7,512]{2,1,0:T(8,128)}) async-done(((f32[512,768]{1,0:T(8,128)}, f32[256,512]{1,0:T(8,128)}, f32[7,7,512]{2,1,0:T(8,128)}), (f32[512,768]{1,0:T(8,128)}, f32[256,512]{1,0:T(8,128)}, f32[7,7,512]{2,1,0:T(8,128)})) %all-reduce.3.cloned.1.call-update) | async-done | bytes 2197520 | tf_op jit(solution)/shard_map/psum | solution.py:171
  222.1 2.7 %copy.139 = f32[512,768]{1,0:T(8,128)} copy(f32[512,768]{1,0:T(8,128)} %get-tuple-element.154) | data formatting | bytes 3145728
  (252 shorter events, 42.2 us)
Async XLA Ops:
  7.2 37.4 %copy-start = (bf16[512,768]{1,0:T(8,128)(2,1)S(1)}, bf16[512,768]{1,0:T(8,128)(2,1)}, u32[]{:S(2)}) copy-start(bf16[512,768]{1,0:T(8,128)(2,1)} %param.10) | copy-start | bytes 2359300
  8.4 12.4 %collective-permute-start = (bf16[1,32,3,512]{3,2,1,0:T(4,128)(2,1)S(1)}, bf16[1,32,3,512]{3,2,1,0:T(4,128)(2,1)S(1)}, u32[]{:S(2)}, u32[]{:S(2)}) collective-permute-start(bf16[1,32,3,512]{3,2,1,0:T(4,128)(2,1)S(1)} %get-tuple-element.93), channel_id=1, source_target_pairs={{0,4},{4,8},{8,12},{12,0},{1,5},{5,9},{9,13},{13,1},{2,6},{6,10},{... | collective-permute-start | bytes 294920 | tf_op jit(solution)/shard_map/ppermute | solution.py:18
  11.6 9.3 %collective-permute-start.1 = (bf16[1,32,3,512]{3,2,1,0:T(4,128)(2,1)S(1)}, bf16[1,32,3,512]{3,2,1,0:T(4,128)(2,1)S(1)}, u32[]{:S(2)}, u32[]{:S(2)}) collective-permute-start(bf16[1,32,3,512]{3,2,1,0:T(4,128)(2,1)S(1)} %get-tuple-element.94), channel_id=1, source_target_pairs={{4,0},{8,4},{12,8},{0,12},{5,1},{9,5},{13,9},{1,13},{6,2},{10,6},{... | collective-permute-start | bytes 294920 | tf_op jit(solution)/shard_map/ppermute | solution.py:19
  15.6 30.2 %all-to-all-start.2 = ((bf16[1,32,8,256]{3,2,0,1:T(8,128)(2,1)}), bf16[1,32,8,256]{3,2,0,1:T(8,128)(2,1)}, u32[]{:S(2)}, u32[]{:S(2)}) async-start(bf16[1,32,8,256]{3,2,0,1:T(8,128)(2,1)} %fusion.15), calls=%async_computation.2 | async-start | bytes 262144 | tf_op jit(solution)/shard_map/all_to_all | solution.py:140
  22.1 5.5 %collective-permute-start.2 = (bf16[1,3,14,512]{3,2,1,0:T(8,128)(2,1)S(1)}, bf16[1,3,14,512]{3,2,1,0:T(8,128)(2,1)S(1)}, u32[]{:S(2)}, u32[]{:S(2)}) collective-permute-start(bf16[1,3,14,512]{3,2,1,0:T(8,128)(2,1)S(1)} %get-tuple-element.84), channel_id=1, source_target_pairs={{0,2},{1,3},{4,6},{5,7},{8,10},{9,11},{12,14},{13,15},{16,18},{17,... | collective-permute-start | bytes 129032 | tf_op jit(solution)/shard_map/ppermute | solution.py:18
  25.7 6.0 %collective-permute-start.3 = (bf16[1,3,14,512]{3,2,1,0:T(8,128)(2,1)S(1)}, bf16[1,3,14,512]{3,2,1,0:T(8,128)(2,1)S(1)}, u32[]{:S(2)}, u32[]{:S(2)}) collective-permute-start(bf16[1,3,14,512]{3,2,1,0:T(8,128)(2,1)S(1)} %get-tuple-element.85), channel_id=1, source_target_pairs={{2,0},{3,1},{6,4},{7,5},{10,8},{11,9},{14,12},{15,13},{18,16},{19,... | collective-permute-start | bytes 129032 | tf_op jit(solution)/shard_map/ppermute | solution.py:19
  45.7 14.6 %all-to-all-start = ((bf16[1,32,8,768]{3,2,0,1:T(8,128)(2,1)}), bf16[1,32,8,768]{3,2,0,1:T(8,128)(2,1)S(1)}, u32[]{:S(2)}, u32[]{:S(2)}) async-start(bf16[1,32,8,768]{3,2,0,1:T(8,128)(2,1)} %fusion.10), calls=%async_computation | async-start | bytes 786432 | tf_op jit(solution)/shard_map/all_to_all | solution.py:123
  75.1 12.5 %all-to-all-start.1 = ((bf16[1,8,32,256]{3,1,0,2:T(8,128)(2,1)}), bf16[1,8,32,256]{3,1,0,2:T(8,128)(2,1)}, u32[]{:S(2)}, u32[]{:S(2)}) async-start(bf16[1,8,32,256]{3,1,0,2:T(8,128)(2,1)} %reshape.619), calls=%async_computation.1 | async-start | bytes 262144 | tf_op jit(solution)/shard_map/all_to_all | solution.py:131
  87.6 13.9 %all-to-all-start.3 = ((bf16[1,8,32,768]{3,1,0,2:T(8,128)(2,1)}), bf16[1,8,32,768]{3,1,0,2:T(8,128)(2,1)S(1)}, u32[]{:S(2)}, u32[]{:S(2)}) async-start(bf16[1,8,32,768]{3,1,0,2:T(8,128)(2,1)} %copy.93), calls=%async_computation.3 | async-start | bytes 786432 | tf_op jit(solution)/shard_map/all_to_all | solution.py:148
  92.7 129.4 %all-reduce.3.cloned.1.call-start = ((), (), s32[]{:S(2)}) async-start(), calls=%async_computation.4 | async-start | bytes 4423680 | tf_op jit(solution)/shard_map/psum | solution.py:171
  107.0 6.9 %collective-permute-start.4 = (bf16[1,32,3,512]{3,2,1,0:T(4,128)(2,1)S(1)}, bf16[1,32,3,512]{3,2,1,0:T(4,128)(2,1)S(1)}, u32[]{:S(2)}, u32[]{:S(2)}) collective-permute-start(bf16[1,32,3,512]{3,2,1,0:T(4,128)(2,1)S(1)} %get-tuple-element.91), channel_id=1, source_target_pairs={{0,4},{4,8},{8,12},{12,0},{1,5},{5,9},{9,13},{13,1},{2,6},{6,10},{... | collective-permute-start | bytes 294920 | tf_op jit(solution)/shard_map/ppermute | solution.py:18
  107.6 6.4 %collective-permute-start.5 = (bf16[1,32,3,512]{3,2,1,0:T(4,128)(2,1)S(1)}, bf16[1,32,3,512]{3,2,1,0:T(4,128)(2,1)S(1)}, u32[]{:S(2)}, u32[]{:S(2)}) collective-permute-start(bf16[1,32,3,512]{3,2,1,0:T(4,128)(2,1)S(1)} %get-tuple-element.92), channel_id=1, source_target_pairs={{4,0},{8,4},{12,8},{0,12},{5,1},{9,5},{13,9},{1,13},{6,2},{10,6},{... | collective-permute-start | bytes 294920 | tf_op jit(solution)/shard_map/ppermute | solution.py:19
  114.1 38.6 %collective-permute-start.6 = (bf16[1,3,14,512]{3,2,1,0:T(8,128)(2,1)S(1)}, bf16[1,3,14,512]{3,2,1,0:T(8,128)(2,1)S(1)}, u32[]{:S(2)}, u32[]{:S(2)}) collective-permute-start(bf16[1,3,14,512]{3,2,1,0:T(8,128)(2,1)S(1)} %get-tuple-element.80), channel_id=1, source_target_pairs={{0,2},{1,3},{4,6},{5,7},{8,10},{9,11},{12,14},{13,15},{16,18},{17,... | collective-permute-start | bytes 129032 | tf_op jit(solution)/shard_map/ppermute | solution.py:18
  116.3 36.4 %collective-permute-start.7 = (bf16[1,3,14,512]{3,2,1,0:T(8,128)(2,1)S(1)}, bf16[1,3,14,512]{3,2,1,0:T(8,128)(2,1)S(1)}, u32[]{:S(2)}, u32[]{:S(2)}) collective-permute-start(bf16[1,3,14,512]{3,2,1,0:T(8,128)(2,1)S(1)} %get-tuple-element.81), channel_id=1, source_target_pairs={{2,0},{3,1},{6,4},{7,5},{10,8},{11,9},{14,12},{15,13},{18,16},{19,... | collective-permute-start | bytes 129032 | tf_op jit(solution)/shard_map/ppermute | solution.py:19
  119.8 32.8 %copy-start.4 = (bf16[1,32,8,512]{3,2,1,0:T(8,128)(2,1)S(1)}, bf16[1,32,8,512]{3,2,1,0:T(8,128)(2,1)}, u32[]{:S(2)}) copy-start(bf16[1,32,8,512]{3,2,1,0:T(8,128)(2,1)} %copy-done.3) | copy-start | bytes 786436
  119.8 32.8 %copy-start.13 = (bf16[1,32,3,512]{3,2,1,0:T(4,128)(2,1)S(1)}, bf16[1,32,3,512]{3,2,1,0:T(4,128)(2,1)}, u32[]{:S(2)}) copy-start(bf16[1,32,3,512]{3,2,1,0:T(4,128)(2,1)} %copy-done.12) | copy-start | bytes 294916
  119.8 32.8 %copy-start.15 = (bf16[1,32,3,512]{3,2,1,0:T(4,128)(2,1)S(1)}, bf16[1,32,3,512]{3,2,1,0:T(4,128)(2,1)}, u32[]{:S(2)}) copy-start(bf16[1,32,3,512]{3,2,1,0:T(4,128)(2,1)} %copy-done.14) | copy-start | bytes 294916
  120.5 32.4 %copy-start.22 = (f32[1,1,512]{2,1,0:T(1,128)S(1)}, f32[1,1,512]{2,1,0:T(1,128)}, u32[]{:S(2)}) copy-start(f32[1,1,512]{2,1,0:T(1,128)} %get-tuple-element.108) | copy-start | bytes 6148
  120.6 32.4 %copy-start.23 = (f32[1,1,512]{2,1,0:T(1,128)S(1)}, f32[1,1,512]{2,1,0:T(1,128)}, u32[]{:S(2)}) copy-start(f32[1,1,512]{2,1,0:T(1,128)} %get-tuple-element.109) | copy-start | bytes 6148
  120.6 32.4 %copy-start.24 = (f32[1,1,512]{2,1,0:T(1,128)S(1)}, f32[1,1,512]{2,1,0:T(1,128)}, u32[]{:S(2)}) copy-start(f32[1,1,512]{2,1,0:T(1,128)} %get-tuple-element.110) | copy-start | bytes 6148
  120.6 32.4 %copy-start.25 = (f32[1,1,512]{2,1,0:T(1,128)S(1)}, f32[1,1,512]{2,1,0:T(1,128)}, u32[]{:S(2)}) copy-start(f32[1,1,512]{2,1,0:T(1,128)} %get-tuple-element.111) | copy-start | bytes 6148
  120.6 32.4 %copy-start.26 = (f32[1,1,512]{2,1,0:T(1,128)S(1)}, f32[1,1,512]{2,1,0:T(1,128)}, u32[]{:S(2)}) copy-start(f32[1,1,512]{2,1,0:T(1,128)} %get-tuple-element.112) | copy-start | bytes 6148
  120.6 32.4 %copy-start.27 = (f32[1,1,512]{2,1,0:T(1,128)S(1)}, f32[1,1,512]{2,1,0:T(1,128)}, u32[]{:S(2)}) copy-start(f32[1,1,512]{2,1,0:T(1,128)} %get-tuple-element.113) | copy-start | bytes 6148
  120.6 32.4 %copy-start.28 = (f32[1,1,512]{2,1,0:T(1,128)S(1)}, f32[1,1,512]{2,1,0:T(1,128)}, u32[]{:S(2)}) copy-start(f32[1,1,512]{2,1,0:T(1,128)} %get-tuple-element.114) | copy-start | bytes 6148
  (84 other events, 1181.3 us)
Sparse Core Ops, SparseCore 0:
  120.7 101.3 all-reduce.2
where the time goes:
time: 234 us; the launch traced here: 233 us
  waiting for transfers between devices  80.2 us (34%)
  starting transfers between devices  35 us (15%)
  blocking collectives  31.5 us (13%)
  local copies, waits for them, and re-layouts  25.9 us (11%)
  other arithmetic  25.8 us (11%)
  matrix products  19.2 us (8%)
  between operations  15.5 us (7%)
    psum x1, waiting for transfers between devices, on_device(): lax.psum((grad_weight, grad_out, grad_conv, grad_gain), ('lon', 'lat', 'd...  64.3 us
    psum x1, blocking collectives, on_device(): lax.psum((grad_weight, grad_out, grad_conv, grad_gain), ('lon', 'lat', 'd...  31.5 us
    reduce_sum x1, other arithmetic, on_device(): inverse = lax.rsqrt(jnp.mean(update * update, -1, keepdims=True) + EPSILON)  10.5 us
    ppermute x4, starting transfers between devices, with_halo(): before = lax.ppermute(last, axis, up)  9.14 us
    ppermute x4, starting transfers between devices, with_halo(): after = lax.ppermute(first, axis, down)  7.95 us
    all_to_all x1, waiting for transfers between devices, on_device(): lax.all_to_all(projected.reshape(batch_count, lat_rows, lon_cols, 3 * att...  6.17 us
    reduce_sum x3, other arithmetic, correlate(): pieces.append(jnp.sum(window * upstream, axis=(0, 1, 2)))  5.91 us
    unnamed x194, local copies, waits for them, and re-layouts  5.57 us
  transfers between devices with their start and end apart: 13, of which 6 were waited for; matrix products, arithmetic and copies ran while one was open for 19% of the time, Pallas kernels for 0%

commit v1 on v0

--- a/solution.py
+++ b/solution.py
@@ -168,7 +168,7 @@
         grad_update + spread(grad_padded, conv_weight[::-1, ::-1], lat_rows, lon_cols)
     ).astype(jnp.bfloat16)
     grad_conv = correlate(padded, grad_update, lat_rows, lon_cols)
-    totals = lax.psum((grad_weight, grad_out, grad_conv, grad_gain), ("lon", "lat", "dp"))
+    totals = lax.psum(lax.psum((grad_weight, grad_out, grad_conv, grad_gain), ("lat", "dp")), "lon")
     return (result, grad_fields, totals[0], totals[1], totals[2], totals[3])
 
 

time: 234 us -> 270 us (1.15)
  waiting for transfers between devices: 80.2 us -> 129 us
  blocking collectives: 31.5 us -> 18.8 us
    psum x1 -> x2, waiting for transfers between devices: 64.3 us -> 106 us  [the longest x1 53.9 us: on_device(): lax.psum(lax.psum((grad_weight, grad_out, grad_conv, grad_gain), ('lat',...]
    psum x1 -> x2, blocking collectives: 31.5 us -> 18.8 us  [the longest x1 11.6 us: on_device(): lax.psum(lax.psum((grad_weight, grad_out, grad_conv, grad_gain), ('lat',...]
    another operation x1, local copies, waits for them, and re-layouts: 0.24 us -> 3.78 us  [correlate(): return jnp.stack(pieces).reshape(7, 7, -1)]
    ppermute x4, waiting for transfers between devices: 1.36 us -> 4.36 us  [with_halo(): before = lax.ppermute(last, axis, up)]
    unnamed x194 -> x166, local copies, waits for them, and re-layouts: 5.57 us -> 5.17 us
  transfers between devices with their start and end apart: 13 -> 14, of which waited for: 6 -> 7; matrix products, arithmetic and copies ran while one was open for 19% -> 13% of each run, Pallas kernels for 0% -> 0%
where the time goes in v1:
time: 270 us; the launch traced here: 268 us
  waiting for transfers between devices  129 us (48%)
  starting transfers between devices  35.8 us (13%)
  other arithmetic  25.4 us (9%)
  local copies, waits for them, and re-layouts  25.2 us (9%)
  matrix products  19.3 us (7%)
  blocking collectives  18.8 us (7%)
  between operations  15.3 us (6%)
    psum x1, waiting for transfers between devices, on_device(): lax.psum(lax.psum((grad_weight, grad_out, grad_conv, grad_gain), ('lat',...  53.9 us
    psum x1, waiting for transfers between devices, on_device(): lax.psum((grad_weight, grad_out, grad_conv, grad_gain), ('lat', 'dp'))  51.7 us
    psum x1, blocking collectives, on_device(): lax.psum(lax.psum((grad_weight, grad_out, grad_conv, grad_gain), ('lat',...  11.6 us
    ppermute x4, starting transfers between devices, with_halo(): before = lax.ppermute(last, axis, up)  10.7 us
    reduce_sum x1, other arithmetic, on_device(): inverse = lax.rsqrt(jnp.mean(update * update, -1, keepdims=True) + EPSILON)  10.5 us
    all_to_all x1, waiting for transfers between devices, on_device(): lax.all_to_all(projected.reshape(batch_count, lat_rows, lon_cols, 3 * att...  8.46 us
    psum x1, blocking collectives, on_device(): lax.psum((grad_weight, grad_out, grad_conv, grad_gain), ('lat', 'dp'))  7.28 us
    ppermute x4, starting transfers between devices, with_halo(): after = lax.ppermute(first, axis, down)  7.01 us
  transfers between devices with their start and end apart: 14, of which 7 were waited for; matrix products, arithmetic and copies ran while one was open for 13% of the time, Pallas kernels for 0%

profile of v1, /device:TPU:0, one launch (start us, length us, event | category | flops | bytes accessed | tf_op | source)
XLA Modules:
  0.0 268.5 jit_solution(944813852257778223)
XLA Ops:
  8.4 3.1 %collective-permute-start = (bf16[1,32,3,512]{3,2,1,0:T(4,128)(2,1)S(1)}, bf16[1,32,3,512]{3,2,1,0:T(4,128)(2,1)S(1)}, u32[]{:S(2)}, u32[]{:S(2)}) collective-permute-start(bf16[1,32,3,512]{3,2,1,0:T(4,128)(2,1)S(1)} %get-tuple-element.96), channel_id=1, source_target_pairs={{0,4},{4,8},{8,12},{12,0},{1,5},{5,9},{9,13},{13,1},{2,6},{6,10},{... | collective-permute-start | bytes 294920 | tf_op jit(solution)/shard_map/ppermute | solution.py:18
  11.6 2.1 collective-permute-start.1
  15.6 3.9 %all-to-all-start.2 = ((bf16[1,32,8,256]{3,2,0,1:T(8,128)(2,1)}), bf16[1,32,8,256]{3,2,0,1:T(8,128)(2,1)}, u32[]{:S(2)}, u32[]{:S(2)}) async-start(bf16[1,32,8,256]{3,2,0,1:T(8,128)(2,1)} %fusion.15), calls=%async_computation.2 | async-start | bytes 262144 | tf_op jit(solution)/shard_map/all_to_all | solution.py:140
  22.2 3.5 %collective-permute-start.2 = (bf16[1,3,14,512]{3,2,1,0:T(8,128)(2,1)S(1)}, bf16[1,3,14,512]{3,2,1,0:T(8,128)(2,1)S(1)}, u32[]{:S(2)}, u32[]{:S(2)}) collective-permute-start(bf16[1,3,14,512]{3,2,1,0:T(8,128)(2,1)S(1)} %get-tuple-element.87), channel_id=1, source_target_pairs={{0,2},{1,3},{4,6},{5,7},{8,10},{9,11},{12,14},{13,15},{16,18},{17,... | collective-permute-start | bytes 129032 | tf_op jit(solution)/shard_map/ppermute | solution.py:18
  27.7 4.0 %collective-permute-done.3 = bf16[1,3,14,512]{3,2,1,0:T(8,128)(2,1)S(1)} collective-permute-done((bf16[1,3,14,512]{3,2,1,0:T(8,128)(2,1)S(1)}, bf16[1,3,14,512]{3,2,1,0:T(8,128)(2,1)S(1)}, u32[]{:S(2)}, u32[]{:S(2)}) %collective-permute-start.3) | collective-permute-done | bytes 43040 | tf_op jit(solution)/shard_map/ppermute | solution.py:19
  34.1 10.5 %multiply_reduce_fusion.51 = (f32[32,8]{1,0:T(8,128)S(1)}, f32[1,32,8,512]{3,2,1,0:T(8,128)S(1)}) fusion(f32[1,32,14,512]{3,2,1,0:T(8,128)S(1)} %get-tuple-element.80, f32[512]{0:T(512)} %bitcast.283, f32[512]{0:T(512)} %bitcast.285, f32[512]{0:T(512)S(1)} %bitcast.191, f32[512]{0:T(512)S(1)} %bitcast.193, f32[512]{0:T(512)S(1)} %bitcast.195, ...), kind=kLoop, calls=%fused_computation.293 | loop fusion | flops 13238016 | bytes 26577920 | tf_op jit(solution)/shard_map/reduce_sum | solution.py:119
  45.8 5.0 %all-to-all-start = ((bf16[1,32,8,768]{3,2,0,1:T(8,128)(2,1)}), bf16[1,32,8,768]{3,2,0,1:T(8,128)(2,1)S(1)}, u32[]{:S(2)}, u32[]{:S(2)}) async-start(bf16[1,32,8,768]{3,2,0,1:T(8,128)(2,1)} %fusion.10), calls=%async_computation | async-start | bytes 786432 | tf_op jit(solution)/shard_map/all_to_all | solution.py:123
  51.9 8.5 %all-to-all-done = bf16[1,32,8,768]{3,2,0,1:T(8,128)(2,1)S(1)} async-done(((bf16[1,32,8,768]{3,2,0,1:T(8,128)(2,1)}), bf16[1,32,8,768]{3,2,0,1:T(8,128)(2,1)S(1)}, u32[]{:S(2)}, u32[]{:S(2)}) %all-to-all-start) | async-done | bytes 393248 | tf_op jit(solution)/shard_map/all_to_all | solution.py:123
  68.6 2.3 fusion.12
  74.2 3.9 %all-to-all-start.1 = ((bf16[1,8,32,256]{3,1,0,2:T(8,128)(2,1)}), bf16[1,8,32,256]{3,1,0,2:T(8,128)(2,1)}, u32[]{:S(2)}, u32[]{:S(2)}) async-start(bf16[1,8,32,256]{3,1,0,2:T(8,128)(2,1)} %reshape.619), calls=%async_computation.1 | async-start | bytes 262144 | tf_op jit(solution)/shard_map/all_to_all | solution.py:131
  78.2 2.3 fusion.13
  84.1 5.1 %all-to-all-start.3 = ((bf16[1,8,32,768]{3,1,0,2:T(8,128)(2,1)}), bf16[1,8,32,768]{3,1,0,2:T(8,128)(2,1)}, u32[]{:S(2)}, u32[]{:S(2)}) async-start(bf16[1,8,32,768]{3,1,0,2:T(8,128)(2,1)} %copy.93), calls=%async_computation.3 | async-start | bytes 786432 | tf_op jit(solution)/shard_map/all_to_all | solution.py:148
  93.1 5.1 %all-to-all-done.3 = bf16[1,8,32,768]{3,1,0,2:T(8,128)(2,1)} async-done(((bf16[1,8,32,768]{3,1,0,2:T(8,128)(2,1)}), bf16[1,8,32,768]{3,1,0,2:T(8,128)(2,1)}, u32[]{:S(2)}, u32[]{:S(2)}) %all-to-all-start.3) | async-done | bytes 393248 | tf_op jit(solution)/shard_map/all_to_all | solution.py:148
  102.0 2.3 multiply_reduce_fusion.2
  108.1 3.8 %stack.199 = f32[49,512]{1,0:T(8,128)S(1)} concatenate(f32[1,512]{1,0:T(1,128)} %bitcast.333, f32[1,512]{1,0:T(1,128)} %bitcast.334, f32[1,512]{1,0:T(1,128)} %bitcast.335, f32[1,512]{1,0:T(1,128)} %bitcast.322, f32[1,512]{1,0:T(1,128)} %bitcast.321, f32[1,512]{1,0:T(1,128)} %bitcast.320, f32[1,512]{1,0:T(1,128)} %bitcast.319, f32[1,512]{1,0:T(1,128)} %bitcast.318, ...), dimensions={0} | concatenate | bytes 200704 | tf_op jit(solution)/shard_map/stack | solution.py:46
  112.7 51.7 %all-reduce.5.cloned.1.call-done = (f32[512,768]{1,0:T(8,128)}, f32[256,512]{1,0:T(8,128)}, f32[7,7,512]{2,1,0:T(8,128)}) async-done(((f32[512,768]{1,0:T(8,128)}, f32[256,512]{1,0:T(8,128)}, f32[7,7,512]{2,1,0:T(8,128)}), (f32[512,768]{1,0:T(8,128)}, f32[256,512]{1,0:T(8,128)}, f32[7,7,512]{2,1,0:T(8,128)})) %all-reduce.5.cloned.1.call-update) | async-done | bytes 2197520 | tf_op jit(solution)/shard_map/psum | solution.py:171
  166.1 2.3 collective-permute-start.5
  168.4 4.4 %collective-permute-done.4 = bf16[1,32,3,512]{3,2,1,0:T(4,128)(2,1)S(1)} collective-permute-done((bf16[1,32,3,512]{3,2,1,0:T(4,128)(2,1)S(1)}, bf16[1,32,3,512]{3,2,1,0:T(4,128)(2,1)S(1)}, u32[]{:S(2)}, u32[]{:S(2)}) %collective-permute-start.4) | collective-permute-done | bytes 98336 | tf_op jit(solution)/shard_map/ppermute | solution.py:18
  173.7 2.5 collective-permute-start.6
  178.9 7.3 %psum.62 = f32[512]{0:T(512)S(1)} all-reduce(f32[512]{0:T(512)} %get-tuple-element.48), channel_id=1, replica_groups=mesh['member'=2,'lon'=4,'lat'=2,'dp'=2] {'lat','dp'}, use_global_device_ids=true, to_apply=%region_61.0 | all-reduce | flops 512 | bytes 4096 | tf_op jit(solution)/shard_map/psum | solution.py:171
  186.2 11.6 %psum.63 = f32[512]{0:T(512)} all-reduce(f32[512]{0:T(512)S(1)} %psum.62), channel_id=1, replica_groups=mesh['member'=2,'lon'=4,'lat'=2,'dp'=2] {'lon'}, use_global_device_ids=true, to_apply=%region_62.0 | all-reduce | flops 512 | bytes 4096 | tf_op jit(solution)/shard_map/psum | solution.py:171
  198.4 5.2 %fusion.24 = bf16[1,32,8,512]{3,2,1,0:T(8,128)(2,1)} fusion(f32[1,32,8,512]{3,2,1,0:T(8,128)S(1)} %get-tuple-element.73, f32[1,38,14,512]{3,2,1,0:T(8,128)S(1)} %maximum_convert_fusion, f32[512]{0:T(512)} %bitcast.284, f32[512]{0:T(512)} %bitcast.286, f32[512]{0:T(512)S(1)} %bitcast.192, f32[512]{0:T(512)S(1)} %bitcast.194, f32[512]{0:T(512)S(1)} %bitcast.196, ...), kind=kLoop, calls=%fused_computation.42 | loop fusion | flops 12976128 | bytes 26576896 | tf_op jit(solution)/shard_map/convert_element_type | solution.py:169
  203.6 53.9 %all-reduce.7.cloned.1.call-done = (f32[512,768]{1,0:T(8,128)}, f32[256,512]{1,0:T(8,128)}, f32[7,7,512]{2,1,0:T(8,128)}) async-done(((f32[512,768]{1,0:T(8,128)}, f32[256,512]{1,0:T(8,128)}, f32[7,7,512]{2,1,0:T(8,128)}), (f32[512,768]{1,0:T(8,128)}, f32[256,512]{1,0:T(8,128)}, f32[7,7,512]{2,1,0:T(8,128)})) %all-reduce.7.cloned.1.call-update) | async-done | bytes 2197520 | tf_op jit(solution)/shard_map/psum | solution.py:171
  257.5 2.7 %copy.142 = f32[512,768]{1,0:T(8,128)} copy(f32[512,768]{1,0:T(8,128)} %get-tuple-element.157) | data formatting | bytes 3145728
  (228 shorter events, 46.1 us)
Async XLA Ops:
  7.2 37.5 %copy-start = (bf16[512,768]{1,0:T(8,128)(2,1)S(1)}, bf16[512,768]{1,0:T(8,128)(2,1)}, u32[]{:S(2)}) copy-start(bf16[512,768]{1,0:T(8,128)(2,1)} %param.10) | copy-start | bytes 2359300
  8.4 12.5 %collective-permute-start = (bf16[1,32,3,512]{3,2,1,0:T(4,128)(2,1)S(1)}, bf16[1,32,3,512]{3,2,1,0:T(4,128)(2,1)S(1)}, u32[]{:S(2)}, u32[]{:S(2)}) collective-permute-start(bf16[1,32,3,512]{3,2,1,0:T(4,128)(2,1)S(1)} %get-tuple-element.96), channel_id=1, source_target_pairs={{0,4},{4,8},{8,12},{12,0},{1,5},{5,9},{9,13},{13,1},{2,6},{6,10},{... | collective-permute-start | bytes 294920 | tf_op jit(solution)/shard_map/ppermute | solution.py:18
  11.6 9.4 %collective-permute-start.1 = (bf16[1,32,3,512]{3,2,1,0:T(4,128)(2,1)S(1)}, bf16[1,32,3,512]{3,2,1,0:T(4,128)(2,1)S(1)}, u32[]{:S(2)}, u32[]{:S(2)}) collective-permute-start(bf16[1,32,3,512]{3,2,1,0:T(4,128)(2,1)S(1)} %get-tuple-element.97), channel_id=1, source_target_pairs={{4,0},{8,4},{12,8},{0,12},{5,1},{9,5},{13,9},{1,13},{6,2},{10,6},{... | collective-permute-start | bytes 294920 | tf_op jit(solution)/shard_map/ppermute | solution.py:19
  15.6 30.2 %all-to-all-start.2 = ((bf16[1,32,8,256]{3,2,0,1:T(8,128)(2,1)}), bf16[1,32,8,256]{3,2,0,1:T(8,128)(2,1)}, u32[]{:S(2)}, u32[]{:S(2)}) async-start(bf16[1,32,8,256]{3,2,0,1:T(8,128)(2,1)} %fusion.15), calls=%async_computation.2 | async-start | bytes 262144 | tf_op jit(solution)/shard_map/all_to_all | solution.py:140
  22.2 5.5 %collective-permute-start.2 = (bf16[1,3,14,512]{3,2,1,0:T(8,128)(2,1)S(1)}, bf16[1,3,14,512]{3,2,1,0:T(8,128)(2,1)S(1)}, u32[]{:S(2)}, u32[]{:S(2)}) collective-permute-start(bf16[1,3,14,512]{3,2,1,0:T(8,128)(2,1)S(1)} %get-tuple-element.87), channel_id=1, source_target_pairs={{0,2},{1,3},{4,6},{5,7},{8,10},{9,11},{12,14},{13,15},{16,18},{17,... | collective-permute-start | bytes 129032 | tf_op jit(solution)/shard_map/ppermute | solution.py:18
  25.8 6.0 %collective-permute-start.3 = (bf16[1,3,14,512]{3,2,1,0:T(8,128)(2,1)S(1)}, bf16[1,3,14,512]{3,2,1,0:T(8,128)(2,1)S(1)}, u32[]{:S(2)}, u32[]{:S(2)}) collective-permute-start(bf16[1,3,14,512]{3,2,1,0:T(8,128)(2,1)S(1)} %get-tuple-element.88), channel_id=1, source_target_pairs={{2,0},{3,1},{6,4},{7,5},{10,8},{11,9},{14,12},{15,13},{18,16},{19,... | collective-permute-start | bytes 129032 | tf_op jit(solution)/shard_map/ppermute | solution.py:19
  45.8 14.6 %all-to-all-start = ((bf16[1,32,8,768]{3,2,0,1:T(8,128)(2,1)}), bf16[1,32,8,768]{3,2,0,1:T(8,128)(2,1)S(1)}, u32[]{:S(2)}, u32[]{:S(2)}) async-start(bf16[1,32,8,768]{3,2,0,1:T(8,128)(2,1)} %fusion.10), calls=%async_computation | async-start | bytes 786432 | tf_op jit(solution)/shard_map/all_to_all | solution.py:123
  74.2 9.9 %all-to-all-start.1 = ((bf16[1,8,32,256]{3,1,0,2:T(8,128)(2,1)}), bf16[1,8,32,256]{3,1,0,2:T(8,128)(2,1)}, u32[]{:S(2)}, u32[]{:S(2)}) async-start(bf16[1,8,32,256]{3,1,0,2:T(8,128)(2,1)} %reshape.619), calls=%async_computation.1 | async-start | bytes 262144 | tf_op jit(solution)/shard_map/all_to_all | solution.py:131
  84.1 14.1 %all-to-all-start.3 = ((bf16[1,8,32,768]{3,1,0,2:T(8,128)(2,1)}), bf16[1,8,32,768]{3,1,0,2:T(8,128)(2,1)}, u32[]{:S(2)}, u32[]{:S(2)}) async-start(bf16[1,8,32,768]{3,1,0,2:T(8,128)(2,1)} %copy.93), calls=%async_computation.3 | async-start | bytes 786432 | tf_op jit(solution)/shard_map/all_to_all | solution.py:148
  89.3 75.1 %all-reduce.5.cloned.1.call-start = ((), (), s32[]{:S(2)}) async-start(), calls=%async_computation.4 | async-start | bytes 4423680 | tf_op jit(solution)/shard_map/psum | solution.py:171
  112.6 144.9 %all-reduce.7.cloned.1.call-start = ((), (), s32[]{:S(2)}) async-start(), calls=%async_computation.5 | async-start | bytes 4423680 | tf_op jit(solution)/shard_map/psum | solution.py:171
  164.5 8.2 %collective-permute-start.4 = (bf16[1,32,3,512]{3,2,1,0:T(4,128)(2,1)S(1)}, bf16[1,32,3,512]{3,2,1,0:T(4,128)(2,1)S(1)}, u32[]{:S(2)}, u32[]{:S(2)}) collective-permute-start(bf16[1,32,3,512]{3,2,1,0:T(4,128)(2,1)S(1)} %get-tuple-element.94), channel_id=1, source_target_pairs={{0,4},{4,8},{8,12},{12,0},{1,5},{5,9},{9,13},{13,1},{2,6},{6,10},{... | collective-permute-start | bytes 294920 | tf_op jit(solution)/shard_map/ppermute | solution.py:18
  166.1 7.6 %collective-permute-start.5 = (bf16[1,32,3,512]{3,2,1,0:T(4,128)(2,1)S(1)}, bf16[1,32,3,512]{3,2,1,0:T(4,128)(2,1)S(1)}, u32[]{:S(2)}, u32[]{:S(2)}) collective-permute-start(bf16[1,32,3,512]{3,2,1,0:T(4,128)(2,1)S(1)} %get-tuple-element.95), channel_id=1, source_target_pairs={{4,0},{8,4},{12,8},{0,12},{5,1},{9,5},{13,9},{1,13},{6,2},{10,6},{... | collective-permute-start | bytes 294920 | tf_op jit(solution)/shard_map/ppermute | solution.py:19
  173.7 24.0 %collective-permute-start.6 = (bf16[1,3,14,512]{3,2,1,0:T(8,128)(2,1)S(1)}, bf16[1,3,14,512]{3,2,1,0:T(8,128)(2,1)S(1)}, u32[]{:S(2)}, u32[]{:S(2)}) collective-permute-start(bf16[1,3,14,512]{3,2,1,0:T(8,128)(2,1)S(1)} %get-tuple-element.83), channel_id=1, source_target_pairs={{0,2},{1,3},{4,6},{5,7},{8,10},{9,11},{12,14},{13,15},{16,18},{17,... | collective-permute-start | bytes 129032 | tf_op jit(solution)/shard_map/ppermute | solution.py:18
  176.3 21.5 %collective-permute-start.7 = (bf16[1,3,14,512]{3,2,1,0:T(8,128)(2,1)S(1)}, bf16[1,3,14,512]{3,2,1,0:T(8,128)(2,1)S(1)}, u32[]{:S(2)}, u32[]{:S(2)}) collective-permute-start(bf16[1,3,14,512]{3,2,1,0:T(8,128)(2,1)S(1)} %get-tuple-element.84), channel_id=1, source_target_pairs={{2,0},{3,1},{6,4},{7,5},{10,8},{11,9},{14,12},{15,13},{18,16},{19,... | collective-permute-start | bytes 129032 | tf_op jit(solution)/shard_map/ppermute | solution.py:19
  177.6 20.4 %copy-start.20 = (f32[1,1,512]{2,1,0:T(1,128)S(1)}, f32[1,1,512]{2,1,0:T(1,128)}, u32[]{:S(2)}) copy-start(f32[1,1,512]{2,1,0:T(1,128)} %copy-done.19) | copy-start | bytes 6148
  177.6 20.4 %copy-start.22 = (f32[1,1,512]{2,1,0:T(1,128)S(1)}, f32[1,1,512]{2,1,0:T(1,128)}, u32[]{:S(2)}) copy-start(f32[1,1,512]{2,1,0:T(1,128)} %copy-done.21) | copy-start | bytes 6148
  177.6 20.4 %copy-start.24 = (f32[1,1,512]{2,1,0:T(1,128)S(1)}, f32[1,1,512]{2,1,0:T(1,128)}, u32[]{:S(2)}) copy-start(f32[1,1,512]{2,1,0:T(1,128)} %copy-done.23) | copy-start | bytes 6148
  177.6 20.4 %copy-start.26 = (f32[1,1,512]{2,1,0:T(1,128)S(1)}, f32[1,1,512]{2,1,0:T(1,128)}, u32[]{:S(2)}) copy-start(f32[1,1,512]{2,1,0:T(1,128)} %copy-done.25) | copy-start | bytes 6148
  177.6 20.4 %copy-start.28 = (f32[1,1,512]{2,1,0:T(1,128)S(1)}, f32[1,1,512]{2,1,0:T(1,128)}, u32[]{:S(2)}) copy-start(f32[1,1,512]{2,1,0:T(1,128)} %copy-done.27) | copy-start | bytes 6148
  177.6 20.4 %copy-start.30 = (f32[1,1,512]{2,1,0:T(1,128)S(1)}, f32[1,1,512]{2,1,0:T(1,128)}, u32[]{:S(2)}) copy-start(f32[1,1,512]{2,1,0:T(1,128)} %copy-done.29) | copy-start | bytes 6148
  177.6 20.4 %copy-start.32 = (f32[1,1,512]{2,1,0:T(1,128)S(1)}, f32[1,1,512]{2,1,0:T(1,128)}, u32[]{:S(2)}) copy-start(f32[1,1,512]{2,1,0:T(1,128)} %copy-done.31) | copy-start | bytes 6148
  177.6 20.4 %copy-start.34 = (f32[1,1,512]{2,1,0:T(1,128)S(1)}, f32[1,1,512]{2,1,0:T(1,128)}, u32[]{:S(2)}) copy-start(f32[1,1,512]{2,1,0:T(1,128)} %copy-done.33) | copy-start | bytes 6148
  177.7 20.4 %copy-start.36 = (f32[1,1,512]{2,1,0:T(1,128)S(1)}, f32[1,1,512]{2,1,0:T(1,128)}, u32[]{:S(2)}) copy-start(f32[1,1,512]{2,1,0:T(1,128)} %copy-done.35) | copy-start | bytes 6148
  (71 other events, 923.2 us)
Sparse Core Ops, SparseCore 0:
  112.7 51.6 all-reduce.4
  167.0 90.4 all-reduce.6
